TPU v7x, 256 devices: a whole 4x4x8 slice. The times are simulated.
256 devices in a mesh: leaf: 32 (over x, z), rows: 8 (over y, core).
Axes of the slice: x: 4, y: 4, z: 8, core: 2. Of those that a mesh axis runs over, the one named last changes fastest.
Arguments:
- child_front_entries: float32 [32, 2, 8, 128, 2048], P('leaf', None, 'rows'), may hold values from 0 to 2, as said below
- parent_fronts: float32 [32, 2, 8, 128, 2048], P('leaf', None, 'rows'), may hold values from 0 to 2, as said below
- parent_of: int32 [32], replicated, may hold values from 0 to 15, never falling along the last dimension, each value on 1 to 4 neighbouring positions
- positions: int32 [32, 8], P('leaf'), may hold values from 0 to 15, as said below
Outputs:
- child_factor: float32 [32, 2, 8, 128, 1024], P('leaf', None, 'rows')
- parent_factor: float32 [32, 2, 8, 128, 1024], P('leaf', None, 'rows')
- parent_contribution_block: float32 [32, 1, 8, 128, 1024], P('leaf', None, 'rows')
Inputs may be any that keep to these rules, and one draw needn't show every extreme that they name: `parent_of`: children of one parent stand at consecutive indices, at most 4 of them, and some parent has exactly 4; every parent has a child. `positions`: each row lists 8 distinct parent block numbers in increasing order; the last is always 16 - 1. `child_front_entries`: each front is symmetric positive definite. `parent_fronts`: each front is symmetric positive definite.
All inputs are finite; a program needn't handle non-finite values.
Results may differ from a plain program's by a relative error of at most 0.000078.
Values sent between devices are 32-bit elements; how exact they have to be, the bound alone decides.
No kernel may reach another device: no remote copies, remote signals or barrier semaphores. Data moves between devices by JAX's collectives and lax.ppermute only.
A program may use at most 256 MiB of HBM per device.

v0:
```python
import jax
import jax.numpy as jnp
from jax import lax
from jax.sharding import PartitionSpec as P

B = 128
PIV = 1024


def entering(x, axis, combine, identity):
    count, position = (lax.axis_size(axis), lax.axis_index(axis))
    everything = jax.tree.map(lambda part: lax.all_gather(part, axis), x)
    start = jax.tree.map(
        lambda part, zero: jnp.broadcast_to(jnp.asarray(zero, part.dtype), part.shape), x, identity
    )

    def turn(k, before):
        at = count - 1 - k
        reached = at > position
        new = combine(before, jax.tree.map(lambda part: part[at], everything))
        return jax.tree.map(lambda a, b: jnp.where(reached, a, b), new, before)

    return lax.fori_loop(0, count, turn, start)


def solve_rows(block_rows, diag_factor):
    return lax.linalg.triangular_solve(
        diag_factor, block_rows, left_side=False, lower=True, transpose_a=True
    )


def settle_blocks(blocks, block_ids, panel_no, diag_factor):
    shaped_ids = block_ids[:, None, None]
    kept = jnp.where(shaped_ids > panel_no, blocks, 0.0)
    return jnp.where(shaped_ids == panel_no, diag_factor[None], kept)


def partial_factor(front_rows, pivot_blocks, kept_blocks):
    front_row_count = lax.axis_size("rows")
    rows_index = lax.axis_index("rows")
    local_blocks = front_rows.shape[0]
    block_size = front_rows.shape[1]
    total_blocks = local_blocks * front_row_count
    pivot_width = pivot_blocks * block_size
    factor_cols = []
    whole_cols = []
    for panel_no in range(pivot_blocks):
        first_col = panel_no * block_size
        column_block = front_rows[:, :, first_col : first_col + block_size]
        if panel_no > 0:
            prior_self = jnp.concatenate(factor_cols, axis=2)
            prior_rows = jnp.concatenate(
                [whole_piece[first_col : first_col + block_size] for whole_piece in whole_cols],
                axis=1,
            )
            column_block = column_block - jnp.einsum(
                "awv,cv->awc", prior_self, prior_rows, precision=lax.Precision.HIGHEST
            )
        gathered = lax.all_gather(column_block[:, None], "rows", axis=1, tiled=True).reshape(
            total_blocks, block_size, block_size
        )
        diag_factor = jnp.linalg.cholesky(gathered[panel_no])
        factor_whole = solve_rows(gathered.reshape(-1, block_size), diag_factor).reshape(
            total_blocks, block_size, block_size
        )
        factor_whole = settle_blocks(
            factor_whole, jnp.arange(total_blocks, dtype=jnp.int32), panel_no, diag_factor
        )
        layered = factor_whole.reshape(local_blocks, front_row_count, block_size, block_size)
        self_front_factor = lax.dynamic_index_in_dim(layered, rows_index, 1, keepdims=False)
        factor_cols.append(self_front_factor)
        whole_cols.append(factor_whole.reshape(-1, block_size))
    self_cols = jnp.concatenate(factor_cols, axis=2)
    whole_factor = jnp.concatenate(whole_cols, axis=1)
    remaining = front_rows[kept_blocks:, :, pivot_width:] - jnp.einsum(
        "awv,cv->awc",
        self_cols[kept_blocks:],
        whole_factor[pivot_width:],
        precision=lax.Precision.HIGHEST,
    )
    return (self_cols, remaining)


def place_rows(update_rows, placement, local_blocks):
    front_row_count = lax.axis_size("rows")
    rows_index = lax.axis_index("rows")
    update_blocks = placement.shape[0]
    local_ids = jnp.arange(local_blocks, dtype=jnp.int32) * front_row_count + rows_index
    block_list = jnp.arange(update_blocks, dtype=jnp.int32)
    piece_rows = lax.all_gather(update_rows[:, None], "rows", axis=1, tiled=True)
    piece_count = piece_rows.shape[1]
    update_ids = (
        jnp.arange(piece_rows.shape[0], dtype=jnp.int32)[:, None] * front_row_count
        + jnp.arange(piece_count, dtype=jnp.int32)[None, :]
    )
    lookup = (update_ids[..., None] == block_list).astype(jnp.int32)
    target_block = jnp.sum(lookup * placement, axis=-1)
    row_onehot = (target_block[None] == local_ids[:, None, None]).astype(jnp.float32)
    return jnp.einsum("phm,hmic->pic", row_onehot, piece_rows, precision=lax.Precision.HIGHEST)


def place_columns(rows_placed, placement_float, front_order):
    local_blocks = rows_placed.shape[0]
    block_size = rows_placed.shape[1]
    update_blocks = placement_float.shape[0]
    col_onehot = (
        placement_float[:, None]
        == jnp.arange(front_order // block_size, dtype=jnp.int32).astype(jnp.float32)[None, :]
    ).astype(jnp.float32)
    shaped = rows_placed.reshape(local_blocks, block_size, update_blocks, block_size)
    placed = jnp.einsum("picb,cq->piqb", shaped, col_onehot, precision=lax.Precision.HIGHEST)
    return placed.reshape(local_blocks, block_size, front_order)


def combine_range(upper_part, lower_part):
    return (
        jnp.maximum(upper_part[0], lower_part[0]),
        lower_part[1] + (1.0 - lower_part[0]) * upper_part[1],
    )


def on_device(child_front_entries, parent_fronts, parent_of, positions):
    front_row_count = lax.axis_size("rows")
    leaf_front_index = lax.axis_index("leaf")
    leaf_count = lax.axis_size("leaf")
    child_front_rows = child_front_entries[0, :, 0]
    local_blocks = child_front_rows.shape[0]
    front_order = child_front_rows.shape[2]
    pivot_blocks = PIV // B
    kept_blocks = pivot_blocks // front_row_count
    child_cols, update_rows = partial_factor(child_front_rows, pivot_blocks, kept_blocks)
    rows_placed = place_rows(update_rows, positions[0], local_blocks)
    own_places = positions[0].astype(jnp.float32)
    extended = place_columns(rows_placed, own_places, front_order)
    leaf_ids = jnp.arange(leaf_count, dtype=jnp.int32)
    previous = jnp.concatenate([jnp.full((1,), -1, jnp.int32), parent_of[:-1]])
    head_flags = (parent_of != previous).astype(jnp.float32)
    head_flag = jnp.sum(jnp.where(leaf_ids == leaf_front_index, head_flags, 0.0))
    carried = entering(
        (head_flag, (1.0 - head_flag) * extended),
        "leaf",
        combine_range,
        (jnp.float32(0.0), jnp.zeros_like(extended)),
    )
    collected = extended + carried[1]
    assembled = parent_fronts[0, :, 0] + collected
    parent_cols, parent_rest = partial_factor(assembled, pivot_blocks, kept_blocks)
    parent_contribution_block = parent_rest * head_flag
    parent_cols = parent_cols * head_flag
    return (
        child_cols[None, :, None],
        parent_cols[None, :, None],
        parent_contribution_block[None, :, None],
    )


def solution(mesh):
    placed = (
        P("leaf", None, "rows", None, None),
        P("leaf", None, "rows", None, None),
        P(),
        P("leaf", None),
    )
    return jax.shard_map(
        on_device,
        mesh=mesh,
        in_specs=placed,
        out_specs=(
            P("leaf", None, "rows", None, None),
            P("leaf", None, "rows", None, None),
            P("leaf", None, "rows", None, None),
        ),
        check_vma=False,
    )
```

profile of v0, /device:TPU:1, one launch (start us, length us, event | category | flops | bytes accessed | tf_op | source)
XLA Modules:
  0.0 1667.4 jit_solution(3161554258178006753)
XLA Ops:
  9.2 31.2 %all-gather.38.cloned.1.call-done = f32[2,1024,128]{2,1,0:T(8,128)} async-done(((f32[2,128,128]{2,1,0:T(8,128)}), f32[2,1024,128]{2,1,0:T(8,128)}) %all-gather.38.cloned.1.call-update) | async-done | bytes 1048592 | tf_op jit(solution)/shard_map/all_gather | solution.py:59
  42.2 11.7 cholesky.254
  74.4 23.4 %all-gather.40.cloned.1.call-done = f32[2,1024,128]{2,1,0:T(8,128)} async-done(((f32[2,128,128]{2,1,0:T(8,128)}), f32[2,1024,128]{2,1,0:T(8,128)}) %all-gather.40.cloned.1.call-update) | async-done | bytes 1048592 | tf_op jit(solution)/shard_map/all_gather | solution.py:59
  99.6 11.7 cholesky.265
  132.9 24.6 %all-gather.42.cloned.1.call-done = f32[2,1024,128]{2,1,0:T(8,128)} async-done(((f32[2,128,128]{2,1,0:T(8,128)}), f32[2,1024,128]{2,1,0:T(8,128)}) %all-gather.42.cloned.1.call-update) | async-done | bytes 1048592 | tf_op jit(solution)/shard_map/all_gather | solution.py:59
  194.5 23.5 %all-gather.44.cloned.1.call-done = f32[2,1024,128]{2,1,0:T(8,128)} async-done(((f32[2,128,128]{2,1,0:T(8,128)}), f32[2,1024,128]{2,1,0:T(8,128)}) %all-gather.44.cloned.1.call-update) | async-done | bytes 1048592 | tf_op jit(solution)/shard_map/all_gather | solution.py:59
  260.8 18.9 %all-gather.46.cloned.1.call-done = f32[2,1024,128]{2,1,0:T(8,128)} async-done(((f32[2,128,128]{2,1,0:T(8,128)}), f32[2,1024,128]{2,1,0:T(8,128)}) %all-gather.46.cloned.1.call-update) | async-done | bytes 1048592 | tf_op jit(solution)/shard_map/all_gather | solution.py:59
  316.5 24.8 %all-gather.48.cloned.1.call-done = f32[2,1024,128]{2,1,0:T(8,128)} async-done(((f32[2,128,128]{2,1,0:T(8,128)}), f32[2,1024,128]{2,1,0:T(8,128)}) %all-gather.48.cloned.1.call-update) | async-done | bytes 1048592 | tf_op jit(solution)/shard_map/all_gather | solution.py:59
  378.5 23.3 %all-gather.50.cloned.1.call-done = f32[2,1024,128]{2,1,0:T(8,128)} async-done(((f32[2,128,128]{2,1,0:T(8,128)}), f32[2,1024,128]{2,1,0:T(8,128)}) %all-gather.50.cloned.1.call-update) | async-done | bytes 1048592 | tf_op jit(solution)/shard_map/all_gather | solution.py:59
  438.0 25.6 %all-gather.52.cloned.1.call-done = f32[2,1024,128]{2,1,0:T(8,128)} async-done(((f32[2,128,128]{2,1,0:T(8,128)}), f32[2,1024,128]{2,1,0:T(8,128)}) %all-gather.52.cloned.1.call-update) | async-done | bytes 1048592 | tf_op jit(solution)/shard_map/all_gather | solution.py:59
  501.3 33.0 %all-gather.54.cloned.1.call-done = f32[8,128,1024]{2,1,0:T(8,128)} async-done(((f32[1,128,1024]{2,1,0:T(8,128)}), f32[8,128,1024]{2,1,0:T(8,128)}) %all-gather.54.cloned.1.call-update) | async-done | bytes 4194320 | tf_op jit(solution)/shard_map/all_gather | solution.py:90
  546.8 63.8 %all-reduce = f32[32]{0:T(128)S(1)} all-reduce(f32[32]{0:T(128)S(1)} %dynamic-update-slice.2), channel_id=1, replica_groups=mesh['leaf'=32,'rows'=8] {'leaf'}, use_global_device_ids=true, to_apply=%add | all-reduce | flops 32 | bytes 256
  613.3 362.3 %all-gather.36.cloned.1.call-done = f32[32,2,128,2048]{3,2,1,0:T(8,128)} async-done(((f32[1,2,128,2048]{3,2,1,0:T(8,128)}), f32[32,2,128,2048]{3,2,1,0:T(8,128)}) %all-gather.36.cloned.1.call-update) | async-done | bytes 67108880 | tf_op jit(solution)/shard_map/all_gather | solution.py:12
  975.6 154.9 %while.16 = (s32[]{:T(128)}, f32[2,128,2048]{2,1,0:T(8,128)S(1)}, s32[]{:T(128)}, f32[32,2,128,2048]{3,2,1,0:T(8,128)}, f32[32]{0:T(128)S(1)}, /*index=5*/s32[]{...) while((s32[]{:T(128)}, f32[2,128,2048]{2,1,0:T(8,128)S(1)}, s32[]{:T(128)}, ...), condition=%wide.region_5.8_spmd.clone, body=%wide.region_4.7_spmd.clone.sunk | while | flops 2097161 | bytes 6291663 | solution.py:23
  1135.5 24.0 %all-gather.56.cloned.1.call-done = f32[2,1024,128]{2,1,0:T(8,128)} async-done(((f32[2,128,128]{2,1,0:T(8,128)}), f32[2,1024,128]{2,1,0:T(8,128)}) %all-gather.56.cloned.1.call-update) | async-done | bytes 1048592 | tf_op jit(solution)/shard_map/all_gather | solution.py:59
  1197.2 24.1 %all-gather.58.cloned.1.call-done = f32[2,1024,128]{2,1,0:T(8,128)} async-done(((f32[2,128,128]{2,1,0:T(8,128)}), f32[2,1024,128]{2,1,0:T(8,128)}) %all-gather.58.cloned.1.call-update) | async-done | bytes 1048592 | tf_op jit(solution)/shard_map/all_gather | solution.py:59
  1257.3 25.7 %all-gather.60.cloned.1.call-done = f32[2,1024,128]{2,1,0:T(8,128)} async-done(((f32[2,128,128]{2,1,0:T(8,128)}), f32[2,1024,128]{2,1,0:T(8,128)}) %all-gather.60.cloned.1.call-update) | async-done | bytes 1048592 | tf_op jit(solution)/shard_map/all_gather | solution.py:59
  1320.8 25.5 %all-gather.62.cloned.1.call-done = f32[2,1024,128]{2,1,0:T(8,128)} async-done(((f32[2,128,128]{2,1,0:T(8,128)}), f32[2,1024,128]{2,1,0:T(8,128)}) %all-gather.62.cloned.1.call-update) | async-done | bytes 1048592 | tf_op jit(solution)/shard_map/all_gather | solution.py:59
  1393.7 17.7 %all-gather.64.cloned.1.call-done = f32[2,1024,128]{2,1,0:T(8,128)} async-done(((f32[2,128,128]{2,1,0:T(8,128)}), f32[2,1024,128]{2,1,0:T(8,128)}) %all-gather.64.cloned.1.call-update) | async-done | bytes 1048592 | tf_op jit(solution)/shard_map/all_gather | solution.py:59
  1415.9 13.2 cholesky.386
  1462.0 25.7 %all-gather.66.cloned.1.call-done = f32[2,1024,128]{2,1,0:T(8,128)} async-done(((f32[2,128,128]{2,1,0:T(8,128)}), f32[2,1024,128]{2,1,0:T(8,128)}) %all-gather.66.cloned.1.call-update) | async-done | bytes 1048592 | tf_op jit(solution)/shard_map/all_gather | solution.py:59
  1530.3 25.5 %all-gather.68.cloned.1.call-done = f32[2,1024,128]{2,1,0:T(8,128)} async-done(((f32[2,128,128]{2,1,0:T(8,128)}), f32[2,1024,128]{2,1,0:T(8,128)}) %all-gather.68.cloned.1.call-update) | async-done | bytes 1048592 | tf_op jit(solution)/shard_map/all_gather | solution.py:59
  1600.6 22.2 %all-gather.70.cloned.1.call-done = f32[2,1024,128]{2,1,0:T(8,128)} async-done(((f32[2,128,128]{2,1,0:T(8,128)}), f32[2,1024,128]{2,1,0:T(8,128)}) %all-gather.70.cloned.1.call-update) | async-done | bytes 1048592 | tf_op jit(solution)/shard_map/all_gather | solution.py:59
  1624.7 11.9 cholesky.419
  (629 shorter events, 734.2 us)
Async XLA Ops:
  7.2 33.3 %all-gather.38.cloned.1.call-start = ((), (), s32[]{:S(2)}) async-start(), calls=%async_computation.1 | async-start | bytes 1179648 | tf_op jit(solution)/shard_map/all_gather | solution.py:59
  8.8 89.0 %all-gather.40.cloned.1.call-start = ((), (), s32[]{:S(2)}) async-start(), calls=%async_computation.2 | async-start | bytes 1179648 | tf_op jit(solution)/shard_map/all_gather | solution.py:59
  9.0 88.9 %copy-start.63 = (pred[2,1]{1,0:T(4,128)(4,1)}, pred[2,1]{1,0:T(4,128)(4,1)S(1)}, u32[]{:S(2)}) copy-start(pred[2,1]{1,0:T(4,128)(4,1)S(1)} %constant_dynamic-slice_fusion.7) | copy-start | bytes 10
  9.0 88.8 %copy-start.65 = (pred[2,1]{1,0:T(4,128)(4,1)}, pred[2,1]{1,0:T(4,128)(4,1)S(1)}, u32[]{:S(2)}) copy-start(pred[2,1]{1,0:T(4,128)(4,1)S(1)} %constant_dynamic-slice_fusion.15) | copy-start | bytes 10
  71.8 85.6 %all-gather.42.cloned.1.call-start = ((), (), s32[]{:S(2)}) async-start(), calls=%async_computation.3 | async-start | bytes 1179648 | tf_op jit(solution)/shard_map/all_gather | solution.py:59
  131.5 86.5 %all-gather.44.cloned.1.call-start = ((), (), s32[]{:S(2)}) async-start(), calls=%async_computation.4 | async-start | bytes 1179648 | tf_op jit(solution)/shard_map/all_gather | solution.py:59
  192.1 87.6 %all-gather.46.cloned.1.call-start = ((), (), s32[]{:S(2)}) async-start(), calls=%async_computation.5 | async-start | bytes 1179648 | tf_op jit(solution)/shard_map/all_gather | solution.py:59
  253.7 87.6 %all-gather.48.cloned.1.call-start = ((), (), s32[]{:S(2)}) async-start(), calls=%async_computation.6 | async-start | bytes 1179648 | tf_op jit(solution)/shard_map/all_gather | solution.py:59
  315.3 86.4 %all-gather.50.cloned.1.call-start = ((), (), s32[]{:S(2)}) async-start(), calls=%async_computation.7 | async-start | bytes 1179648 | tf_op jit(solution)/shard_map/all_gather | solution.py:59
  375.7 87.8 %all-gather.52.cloned.1.call-start = ((), (), s32[]{:S(2)}) async-start(), calls=%async_computation.8 | async-start | bytes 1179648 | tf_op jit(solution)/shard_map/all_gather | solution.py:59
  437.6 96.7 %all-gather.54.cloned.1.call-start = ((), (), s32[]{:S(2)}) async-start(), calls=%async_computation.9 | async-start | bytes 4718592 | tf_op jit(solution)/shard_map/all_gather | solution.py:90
  499.5 476.1 %all-gather.36.cloned.1.call-start = ((), (), s32[]{:S(2)}) async-start(), calls=%async_computation | async-start | bytes 69206016 | tf_op jit(solution)/shard_map/all_gather | solution.py:12
  544.7 614.8 %all-gather.56.cloned.1.call-start = ((), (), s32[]{:S(2)}) async-start(), calls=%async_computation.10 | async-start | bytes 1179648 | tf_op jit(solution)/shard_map/all_gather | solution.py:59
  1135.3 86.0 %all-gather.58.cloned.1.call-start = ((), (), s32[]{:S(2)}) async-start(), calls=%async_computation.11 | async-start | bytes 1179648 | tf_op jit(solution)/shard_map/all_gather | solution.py:59
  1195.3 87.6 %all-gather.60.cloned.1.call-start = ((), (), s32[]{:S(2)}) async-start(), calls=%async_computation.12 | async-start | bytes 1179648 | tf_op jit(solution)/shard_map/all_gather | solution.py:59
  1257.0 89.3 %all-gather.62.cloned.1.call-start = ((), (), s32[]{:S(2)}) async-start(), calls=%async_computation.13 | async-start | bytes 1179648 | tf_op jit(solution)/shard_map/all_gather | solution.py:59
  1320.3 91.1 %all-gather.64.cloned.1.call-start = ((), (), s32[]{:S(2)}) async-start(), calls=%async_computation.14 | async-start | bytes 1179648 | tf_op jit(solution)/shard_map/all_gather | solution.py:59
  1385.4 102.3 %all-gather.66.cloned.1.call-start = ((), (), s32[]{:S(2)}) async-start(), calls=%async_computation.15 | async-start | bytes 1179648 | tf_op jit(solution)/shard_map/all_gather | solution.py:59
  1447.9 68.0 %copy-start.39 = (pred[2048]{0:T(1024)(128)(4,1)S(1)}, pred[2048]{0:T(1024)(128)(4,1)}, u32[]{:S(2)}) copy-start(pred[2048]{0:T(1024)(128)(4,1)} %copy-done.38) | copy-start | bytes 6148
  1447.9 68.0 %copy-start.41 = (pred[2048]{0:T(1024)(128)(4,1)S(1)}, pred[2048]{0:T(1024)(128)(4,1)}, u32[]{:S(2)}) copy-start(pred[2048]{0:T(1024)(128)(4,1)} %copy-done.40) | copy-start | bytes 6148
  1461.7 94.1 %all-gather.68.cloned.1.call-start = ((), (), s32[]{:S(2)}) async-start(), calls=%async_computation.16 | async-start | bytes 1179648 | tf_op jit(solution)/shard_map/all_gather | solution.py:59
  1516.0 68.1 %copy-start.42 = (pred[2048]{0:T(1024)(128)(4,1)S(1)}, pred[2048]{0:T(1024)(128)(4,1)}, u32[]{:S(2)}) copy-start(pred[2048]{0:T(1024)(128)(4,1)} %get-tuple-element.375) | copy-start | bytes 6148
  1516.0 68.1 %copy-start.43 = (pred[2048]{0:T(1024)(128)(4,1)S(1)}, pred[2048]{0:T(1024)(128)(4,1)}, u32[]{:S(2)}) copy-start(pred[2048]{0:T(1024)(128)(4,1)} %get-tuple-element.376) | copy-start | bytes 6148
  1529.8 93.1 %all-gather.70.cloned.1.call-start = ((), (), s32[]{:S(2)}) async-start(), calls=%async_computation.17 | async-start | bytes 1179648 | tf_op jit(solution)/shard_map/all_gather | solution.py:59
  (64 other events, 2414.0 us)
Sparse Core Ops, SparseCore 0:
  10.4 29.9 all-gather.37
  72.0 25.8 all-gather.39
  131.6 25.8 all-gather.41
  192.2 25.8 all-gather.43
  253.8 25.8 all-gather.45
  315.5 25.7 all-gather.47
  375.9 25.8 all-gather.49
  437.7 25.7 all-gather.51
  499.6 34.6 all-gather.53
  544.8 430.7 all-gather.35
  1135.4 24.0 all-gather.55
  1195.5 25.8 all-gather.57
  1257.1 25.8 all-gather.59
  1320.4 25.8 all-gather.61
  1385.5 25.8 all-gather.63
  1461.9 25.8 all-gather.65
  1529.9 25.8 all-gather.67
  1597.0 25.8 all-gather.69
where the time goes:
time: 1680 us; the launch traced here: 1670 us
  waiting for transfers between devices  781 us (46%)
  other arithmetic  538 us (32%)
  local copies, waits for them, and re-layouts  132 us (8%)
  matrix products  108 us (6%)
  blocking collectives  63.8 us (4%)
  loops' own time  23.1 us (1%)
  between operations  17 us (1%)
    all_gather x16, waiting for transfers between devices, partial_factor(): lax.all_gather(column_block[:, None], 'rows', axis=1, tiled=True)  386 us
    all_gather x1, waiting for transfers between devices, entering(): everything = jax.tree.map(lambda part: lax.all_gather(part, axis), x)  362 us
    another operation x48, other arithmetic, partial_factor(): diag_factor = jnp.linalg.cholesky(gathered[panel_no])  201 us
    another operation x32, other arithmetic, solve_rows(): lax.linalg.triangular_solve(diag_factor, block_rows, left_side=False, low...  175 us
    select_n x32, other arithmetic, turn(): return jax.tree.map(lambda a, b: jnp.where(reached, a, b), new, before)  110 us
    unnamed x1, blocking collectives  63.8 us
    another operation x16, matrix products, solve_rows(): lax.linalg.triangular_solve(diag_factor, block_rows, left_side=False, low...  55.9 us
    unnamed x206, local copies, waits for them, and re-layouts  37.3 us
  transfers between devices with their start and end apart: 18, of which 18 were waited for; matrix products, arithmetic and copies ran while one was open for 2% of the time, Pallas kernels for 0%

commit v1 on v0

v1 whole, which is shorter than its diff:
```python
import jax
import jax.numpy as jnp
from jax import lax
from jax.experimental import pallas as pl
from jax.experimental.pallas import tpu as pltpu
from jax.sharding import PartitionSpec as P

B = 128
PIV = 1024
NB = PIV // B
MIB = 2**20
DN = (((1,), (1,)), ((), ()))

def split(x):
    hi = x.astype(jnp.bfloat16)
    lo = (x - hi.astype(jnp.float32)).astype(jnp.bfloat16)
    return hi, lo

def dot(a, b):
    return lax.dot_general(a, b, DN, preferred_element_type=jnp.float32)

def mm(a, b):
    (ah, al), (bh, bl) = a, b
    return dot(ah, bh) + (dot(ah, bl) + dot(al, bh))

def wide(x):
    return jnp.broadcast_to(x, (8, B))

def diag_factor(a_ref, e_ref, u_ref, v_ref):
    sub = lax.broadcasted_iota(jnp.int32, (8, B), 0)
    rows = lax.broadcasted_iota(jnp.int32, (B, B), 0)
    cols = lax.broadcasted_iota(jnp.int32, (B, B), 1)
    e_ref[...] = jnp.where(rows == cols, 1.0, 0.0)

    def panel(p, _):
        v = a_ref[0:8, :]
        er = e_ref[0:8, :]
        c = [wide(v[:, j:j + 1]) for j in range(8)]
        s = [[wide(c[j][i:i + 1, :]) if i >= j else None for j in range(8)] for i in range(8)]
        rolled = pltpu.roll(v, B - 8, 1)
        vr = [wide(rolled[j:j + 1, :]) for j in range(8)]
        ev = [wide(er[j:j + 1, :]) for j in range(8)]
        r = [None] * 8
        for j in range(8):
            r[j] = lax.rsqrt(s[j][j])
            for i in range(j + 1, 8):
                s[i][j] = s[i][j] * r[j]
            for k in range(j + 1, 8):
                for i in range(k, 8):
                    s[i][k] = s[i][k] - s[i][j] * s[k][j]
            vr[j] = vr[j] * r[j]
            ev[j] = ev[j] * r[j]
            for i in range(j + 1, 8):
                vr[i] = vr[i] - s[i][j] * vr[j]
                ev[i] = ev[i] - s[i][j] * ev[j]
        urows, erows = vr[0], ev[0]
        for j in range(1, 8):
            urows = jnp.where(sub == j, vr[j], urows)
            erows = jnp.where(sub == j, ev[j], erows)
        at = pl.multiple_of(p * 8, 8)
        u_ref[pl.ds(at, 8), :] = pltpu.roll(urows, p * 8 + 8, 1)
        v_ref[pl.ds(at, 8), :] = erows
        w, we = list(vr), list(ev)
        for j in range(7, -1, -1):
            w[j] = w[j] * r[j]
            we[j] = we[j] * r[j]
            for k in range(j):
                w[k] = w[k] - s[j][k] * w[j]
                we[k] = we[k] - s[j][k] * we[j]
        for q in range(1, 16):
            aq = a_ref[8 * q:8 * q + 8, :]
            eq = e_ref[8 * q:8 * q + 8, :]
            cq = [wide(aq[:, j:j + 1]) for j in range(8)]
            ar = pltpu.roll(aq, B - 8, 1)
            for j in range(8):
                ar = ar - cq[j] * w[j]
                eq = eq - cq[j] * we[j]
            a_ref[8 * q - 8:8 * q, :] = ar
            e_ref[8 * q - 8:8 * q, :] = eq
        return 0

    lax.fori_loop(0, 16, panel, 0)
    u_ref[...] = jnp.where(cols >= rows, u_ref[...], 0.0)

def chol_kernel(g_ref, l_ref, dinv_ref, s_ref, hi_ref, lo_ref, a_ref, e_ref, u_ref, v_ref):
    for k in range(NB):
        k0, k1 = k * B, k * B + B
        if k == 0:
            for i in range(NB):
                s_ref[i * B:i * B + B, :] = g_ref[i, :, :]
                l_ref[i * B:i * B + B, :] = jnp.zeros((B, NB * B), jnp.float32)
        a_ref[...] = s_ref[k0:k1, k0:k1]
        diag_factor(a_ref, e_ref, u_ref, v_ref)
        l_ref[k0:k1, k0:k1] = u_ref[...].T
        inv = v_ref[...]
        dinv_ref[k] = inv
        if k + 1 < NB:
            n = NB * B - k1
            x = mm(split(s_ref[k1:, k0:k1]), split(inv))
            l_ref[k1:, k0:k1] = x
            h, l = split(x)
            hi_ref[k1:, :] = h
            lo_ref[k1:, :] = l
            for j in range(k + 1, NB):
                j0 = j * B
                s_ref[j0:, j0:j0 + B] = s_ref[j0:, j0:j0 + B] - mm(
                    (hi_ref[j0:, :], lo_ref[j0:, :]), (hi_ref[j0:j0 + B, :], lo_ref[j0:j0 + B, :]))

def chol(g):
    return pl.pallas_call(
        chol_kernel,
        out_shape=(
            jax.ShapeDtypeStruct((PIV, PIV), jnp.float32),
            jax.ShapeDtypeStruct((NB, B, B), jnp.float32),
        ),
        scratch_shapes=[
            pltpu.VMEM((PIV, PIV), jnp.float32),
            pltpu.VMEM((PIV, B), jnp.bfloat16),
            pltpu.VMEM((PIV, B), jnp.bfloat16),
        ]
        + [pltpu.VMEM((B, B), jnp.float32)] * 4,
        compiler_params=pltpu.CompilerParams(vmem_limit_bytes=40 * MIB),
        cost_estimate=pl.CostEstimate(flops=60 * 10**9, bytes_accessed=8 * MIB, transcendentals=0),
        name="chol",
    )(g)


def solve_below(l_ref, dinv_ref, rp_ref, xh_ref, xl_ref):
    for k in range(NB):
        k0, k1 = k * B, k * B + B
        c = rp_ref[:, :, k0:k1].reshape(PIV, B)
        if k > 0:
            c = c - mm((xh_ref[:, :k0], xl_ref[:, :k0]), split(l_ref[k0:k1, :k0]))
        h, l = split(mm(split(c), split(dinv_ref[k])))
        xh_ref[:, k0:k1] = h
        xl_ref[:, k0:k1] = l


def rows_at(ref, block):
    return ref[pl.ds(pl.multiple_of(block * B, B), B), :]


def child_kernel(meta_ref, l_ref, dinv_ref, rp_ref, rr_ref, fac_ref, ep_ref, er_ref, xh_ref, xl_ref):
    solve_below(l_ref, dinv_ref, rp_ref, xh_ref, xl_ref)
    me = meta_ref[0]
    fac_ref[0] = rows_at(l_ref, me)
    fac_ref[1] = rows_at(xh_ref, me).astype(jnp.float32) + rows_at(xl_ref, me).astype(jnp.float32)
    x = (xh_ref[...], xl_ref[...])
    for half, out_ref in ((0, ep_ref), (1, er_ref)):
        a = jnp.int32(-1)
        for b in range(NB):
            a = jnp.where(meta_ref[1 + b] == me + half * NB, b, a)
        held = a >= 0
        a = jnp.maximum(a, 0)
        u = rr_ref[a] - mm((rows_at(xh_ref, a), rows_at(xl_ref, a)), x)
        u = jnp.where(held, u, 0.0)
        out_ref[...] = jnp.zeros_like(out_ref)
        for b in range(NB):
            at = meta_ref[1 + b]
            if half == 0:
                @pl.when(at < NB)
                def _():
                    out_ref[:, pl.ds(pl.multiple_of(at * B, B), B)] = u[:, b * B:b * B + B]
            else:
                out_ref[:, pl.ds(pl.multiple_of(at * B, B), B)] = u[:, b * B:b * B + B]


def parent_kernel(meta_ref, l_ref, dinv_ref, rp_ref, rr_ref, fac_ref, cb_ref, xh_ref, xl_ref):
    solve_below(l_ref, dinv_ref, rp_ref, xh_ref, xl_ref)
    me = meta_ref[0]
    keep = meta_ref[9] > 0
    fac_ref[0] = jnp.where(keep, rows_at(l_ref, me), 0.0)
    xh, xl = rows_at(xh_ref, me), rows_at(xl_ref, me)
    fac_ref[1] = jnp.where(keep, xh.astype(jnp.float32) + xl.astype(jnp.float32), 0.0)
    u = rr_ref[...] - mm((xh, xl), (xh_ref[...], xl_ref[...]))
    cb_ref[...] = jnp.where(keep, u, 0.0)


def tail(kernel, name, outs, *args):
    return pl.pallas_call(
        kernel,
        in_specs=[pl.BlockSpec(memory_space=pltpu.SMEM)] + [pl.BlockSpec(memory_space=pltpu.VMEM)] * 4,
        out_shape=tuple(jax.ShapeDtypeStruct(s, jnp.float32) for s in outs),
        scratch_shapes=[pltpu.VMEM((PIV, PIV), jnp.bfloat16)] * 2,
        compiler_params=pltpu.CompilerParams(vmem_limit_bytes=40 * MIB),
        cost_estimate=pl.CostEstimate(flops=10 * 10**9, bytes_accessed=16 * MIB, transcendentals=0),
        name=name,
    )(*args)


def from_right(x, shift, same):
    leaves = lax.axis_size("leaf")
    got = lax.ppermute(x, "leaf", [(i + shift, i) for i in range(leaves - shift)])
    return x + jnp.where(same, got, 0.0)


def on_device(child_front_entries, parent_fronts, parent_of, positions):
    me = lax.axis_index("rows")
    leaf = lax.axis_index("leaf")
    child = child_front_entries[0, :, 0]
    parent = parent_fronts[0, :, 0]

    leaves = lax.axis_size("leaf")
    padded = jnp.concatenate([jnp.full((1,), -1, jnp.int32), parent_of, jnp.full((2,), -1, jnp.int32)])
    near = lax.dynamic_slice(padded, (leaf,), (4,))
    head = near[1] != near[0]
    same1, same2 = near[1] == near[2], near[1] == near[3]
    meta = jnp.concatenate(
        [me.astype(jnp.int32)[None], positions[0], head.astype(jnp.int32)[None]]
    )

    pp = lax.all_gather(child[0, :, :PIV], "rows")
    rp = lax.all_gather(child[1, :, :PIV], "rows")
    rr = lax.all_gather(child[1, :, PIV:], "rows")
    l, dinv = chol(pp)
    child_out, ext_p, ext_r = tail(
        child_kernel, "child_tail", ((2, B, PIV), (B, PIV), (B, 2 * PIV)), meta, l, dinv, rp, rr
    )
    sum_p = from_right(from_right(ext_p, 1, same1), 2, same2)
    sum_r = from_right(from_right(ext_r, 1, same1), 2, same2)
    pp = lax.all_gather(parent[0, :, :PIV] + sum_p, "rows")
    low = parent[1] + sum_r
    rp = lax.all_gather(low[:, :PIV], "rows")
    l, dinv = chol(pp)
    parent_out, block_out = tail(
        parent_kernel, "parent_tail", ((2, B, PIV), (B, PIV)), meta, l, dinv, rp, low[:, PIV:]
    )
    return (
        child_out[None, :, None],
        parent_out[None, :, None],
        block_out[None, None, None],
    )


def solution(mesh):
    placed = P("leaf", None, "rows", None, None)
    return jax.shard_map(
        on_device,
        mesh=mesh,
        in_specs=(placed, placed, P(), P("leaf", None)),
        out_specs=(placed, placed, placed),
        check_vma=False,
    )
```

time: 1680 us -> 354 us (0.21)
  waiting for transfers between devices: 781 us -> 162 us
  other arithmetic: 538 us -> 2.48 us
  Pallas kernels: 0 us -> 138 us
  local copies, waits for them, and re-layouts: 132 us -> 21.3 us
  matrix products: 108 us -> 0 us
  blocking collectives: 63.8 us -> 0 us
  loops' own time: 23.1 us -> 0 us
    all_gather x18 -> x5, waiting for transfers between devices: 781 us -> 53.6 us  [the longest x1 35.8 us: on_device(): pp = lax.all_gather(child[0, :, :PIV], 'rows')]
    another operation x80 -> x0, other arithmetic: 375 us -> none  [the longest x48 201 us: partial_factor(): diag_factor = jnp.linalg.cholesky(gathered[panel_no])]
    select_n x60 -> x0, other arithmetic: 139 us -> none  [the longest x32 110 us: turn(): return jax.tree.map(lambda a, b: jnp.where(reached, a, b), new, before)]
    pallas_call x0 -> x4, Pallas kernels: none -> 138 us  [the longest x2 104 us: chol(): pl.pallas_call(chol_kernel, out_shape=(jax.ShapeDtypeStruct((PIV, PIV), j...]
    ppermute x0 -> x4, waiting for transfers between devices: none -> 107 us  [from_right(): lax.ppermute(x, 'leaf', [(i + shift, i) for i in range(leaves - shift)])]
    unnamed x1 -> x0, blocking collectives: 63.8 us -> none
    another operation x16 -> x0, matrix products: 55.9 us -> none  [solve_rows(): lax.linalg.triangular_solve(diag_factor, block_rows, left_side=False, low...]
    dot_general x18 -> x0, matrix products: 51.7 us -> none  [the longest x14 31 us: partial_factor(): jnp.einsum('awv,cv->awc', prior_self, prior_rows, precision=lax.Precision...]
  transfers between devices with their start and end apart: 18 -> 9, of which waited for: 18 -> 6; matrix products, arithmetic and copies ran while one was open for 2% -> 1% of each run, Pallas kernels for 0% -> 30%
where the time goes in v1:
time: 354 us; the launch traced here: 348 us
  waiting for transfers between devices  162 us (46%)
  Pallas kernels  138 us (39%)
  local copies, waits for them, and re-layouts  21.3 us (6%)
  between operations  17.7 us (5%)
  starting transfers between devices  5.72 us (2%)
    ppermute x4, waiting for transfers between devices, from_right(): lax.ppermute(x, 'leaf', [(i + shift, i) for i in range(leaves - shift)])  107 us
    pallas_call x2, Pallas kernels, chol(): pl.pallas_call(chol_kernel, out_shape=(jax.ShapeDtypeStruct((PIV, PIV), j...  104 us
    all_gather x1, waiting for transfers between devices, on_device(): pp = lax.all_gather(child[0, :, :PIV], 'rows')  35.8 us
    pallas_call x2, Pallas kernels, tail(): pl.pallas_call(kernel, in_specs=[pl.BlockSpec(memory_space=pltpu.SMEM)] +...  34.3 us
    all_gather x1, waiting for transfers between devices, on_device(): rr = lax.all_gather(child[1, :, PIV:], 'rows')  17.8 us
    unnamed x22, local copies, waits for them, and re-layouts  17.1 us
  transfers between devices with their start and end apart: 9, of which 6 were waited for; matrix products, arithmetic and copies ran while one was open for 1% of the time, Pallas kernels for 30%

profile of v1, /device:TPU:1, one launch (start us, length us, event | category | flops | bytes accessed | tf_op | source)
XLA Modules:
  0.0 347.5 jit_solution(7999070533653356537)
XLA Ops:
  7.2 2.5 fusion.1
  13.5 35.8 %all-gather.8.cloned.1.call-done.g_ref = f32[8,128,1024]{2,1,0:T(8,128)} async-done(((f32[1,128,1024]{2,1,0:T(8,128)}), f32[8,128,1024]{2,1,0:T(8,128)}) %all-gather.8.cloned.1.call-update) | async-done | bytes 4194320 | tf_op jit(solution)/shard_map/all_gather | solution.py:212
  49.3 2.2 copy-done.1
  51.5 52.1 %chol.2 = (f32[1024,1024]{1,0:T(8,128)S(1)}, f32[8,128,128]{2,1,0:T(8,128)S(1)}) custom-call(f32[8,128,1024]{2,1,0:T(8,128)S(1)} %copy-done.1), custom_call_target="tpu_custom_call" | custom-call | flops 60000002048 | bytes 8388608 | tf_op jit(solution)/shard_map/chol/pallas_call | solution.py:110
  103.6 2.0 copy-done.4
  105.6 17.8 %all-gather.12.cloned.1.call-done.rr_ref = f32[8,128,1024]{2,1,0:T(8,128)} async-done(((f32[1,128,1024]{2,1,0:T(8,128)}), f32[8,128,1024]{2,1,0:T(8,128)}) %all-gather.12.cloned.1.call-update) | async-done | bytes 4194320 | tf_op jit(solution)/shard_map/all_gather | solution.py:214
  123.4 2.2 copy-done
  125.6 2.2 copy-done.5
  127.8 18.3 %child_tail.1 = (f32[2,128,1024]{2,1,0:T(8,128)}, f32[128,1024]{1,0:T(8,128)S(1)}, f32[128,2048]{1,0:T(8,128)S(1)}) custom-call(s32[10]{0:T(128)S(1)} %pad_add_fusion.1.meta_ref, f32[1024,1024]{1,0:T(8,128)S(1)} %copy-done.5, f32[8,128,128]{2,1,0:T(8,128)S(1)} %get-tuple-element.13.dinv_ref, f32[8,128,1024]{2,1,0:T(8,128)S(1)} %copy-done, ...), custom_call_target="tpu_custom_call" | custom-call | flops 10000000000 | bytes 16777216 | tf_op jit(solution)/shard_map/child_tail/pallas_call | solution.py:180
  146.1 1.4 collective-permute-start
  148.8 12.5 %collective-permute-done = f32[128,1024]{1,0:T(8,128)S(1)} collective-permute-done((f32[128,1024]{1,0:T(8,128)S(1)}, f32[128,1024]{1,0:T(8,128)S(1)}, u32[]{:S(2)}, u32[]{:S(2)}) %collective-permute-start) | collective-permute-done | bytes 524320 | tf_op jit(solution)/shard_map/ppermute | solution.py:193
  161.4 1.3 collective-permute-start.1
  163.9 23.8 %collective-permute-done.1 = f32[128,1024]{1,0:T(8,128)S(1)} collective-permute-done((f32[128,1024]{1,0:T(8,128)S(1)}, f32[128,1024]{1,0:T(8,128)S(1)}, u32[]{:S(2)}, u32[]{:S(2)}) %collective-permute-start.1) | collective-permute-done | bytes 524320 | tf_op jit(solution)/shard_map/ppermute | solution.py:193
  187.8 2.0 fusion
  189.8 1.3 collective-permute-start.2
  191.1 23.4 %collective-permute-done.2 = f32[128,2048]{1,0:T(8,128)S(1)} collective-permute-done((f32[128,2048]{1,0:T(8,128)S(1)}, f32[128,2048]{1,0:T(8,128)S(1)}, u32[]{:S(2)}, u32[]{:S(2)}) %collective-permute-start.2) | collective-permute-done | bytes 1048608 | tf_op jit(solution)/shard_map/ppermute | solution.py:193
  214.6 1.5 collective-permute-start.3
  216.2 47.2 %collective-permute-done.3 = f32[128,2048]{1,0:T(8,128)S(1)} collective-permute-done((f32[128,2048]{1,0:T(8,128)S(1)}, f32[128,2048]{1,0:T(8,128)S(1)}, u32[]{:S(2)}, u32[]{:S(2)}) %collective-permute-start.3) | collective-permute-done | bytes 1048608 | tf_op jit(solution)/shard_map/ppermute | solution.py:193
  264.5 2.2 copy-done.2
  266.7 52.0 %chol.3 = (f32[1024,1024]{1,0:T(8,128)S(1)}, f32[8,128,128]{2,1,0:T(8,128)S(1)}) custom-call(f32[8,128,1024]{2,1,0:T(8,128)S(1)} %bitcast.21), custom_call_target="tpu_custom_call" | custom-call | flops 60000002048 | bytes 8388608 | tf_op jit(solution)/shard_map/chol/pallas_call | solution.py:110
  318.7 2.0 copy-done.6
  320.6 2.2 copy-done.3
  322.8 2.2 copy-done.7
  325.0 16.0 %parent_tail.1 = (f32[2,128,1024]{2,1,0:T(8,128)}, f32[128,1024]{1,0:T(8,128)}) custom-call(s32[10]{0:T(128)S(1)} %pad_add_fusion.1.meta_ref, f32[1024,1024]{1,0:T(8,128)S(1)} %copy-done.7, f32[8,128,128]{2,1,0:T(8,128)S(1)} %get-tuple-element.17.dinv_ref, f32[8,128,1024]{2,1,0:T(8,128)S(1)} %bitcast.22, f32[128,1024]{1,0:T(8,128)S(1)} %get-tuple-element.30.rr_ref), custom_call_target="tpu_custom_call" | custom-call | flops 10000000000 | bytes 16777216 | tf_op jit(solution)/shard_map/parent_tail/pallas_call | solution.py:180
  (36 shorter events, 3.8 us)
Async XLA Ops:
  7.2 4.2 %copy-start.9 = (s32[32]{0:T(128)S(1)}, s32[32]{0:T(128)}, u32[]{:S(2)}) copy-start(s32[32]{0:T(128)} %param.6) | copy-start | bytes 388
  7.2 6.2 %copy-start.10 = (s32[1,8]{1,0:T(1,128)S(1)}, s32[1,8]{1,0:T(1,128)}, u32[]{:S(2)}) copy-start(s32[1,8]{1,0:T(1,128)} %param.7) | copy-start | bytes 100
  7.2 42.1 %all-gather.8.cloned.1.call-start = ((), (), s32[]{:S(2)}) async-start(), calls=%async_computation | async-start | bytes 4718592 | tf_op jit(solution)/shard_map/all_gather | solution.py:212
  9.8 95.8 %all-gather.10.cloned.1.call-start = ((), (), s32[]{:S(2)}) async-start(), calls=%async_computation.1 | async-start | bytes 4718592 | tf_op jit(solution)/shard_map/all_gather | solution.py:213
  10.6 112.8 %all-gather.12.cloned.1.call-start = ((), (), s32[]{:S(2)}) async-start(), calls=%async_computation.2 | async-start | bytes 4718592 | tf_op jit(solution)/shard_map/all_gather | solution.py:214
  11.3 253.2 %all-gather.14.cloned.1.call-start = ((), (), s32[]{:S(2)}) async-start(), calls=%async_computation.3 | async-start | bytes 4718592 | tf_op jit(solution)/shard_map/all_gather | solution.py:221
  49.3 2.2 copy-start.1
  103.6 2.0 copy-start.4
  123.4 2.2 copy-start
  125.6 2.2 copy-start.5
  146.0 117.3 %copy-start.8 = (f32[1,2,1,128,2048]{4,3,2,1,0:T(8,128)S(1)}, f32[1,2,1,128,2048]{4,3,2,1,0:T(8,128)}, u32[]{:S(2)}) copy-start(f32[1,2,1,128,2048]{4,3,2,1,0:T(8,128)} %param.5) | copy-start | bytes 6291460
  146.1 15.2 %collective-permute-start = (f32[128,1024]{1,0:T(8,128)S(1)}, f32[128,1024]{1,0:T(8,128)S(1)}, u32[]{:S(2)}, u32[]{:S(2)}) collective-permute-start(f32[128,1024]{1,0:T(8,128)S(1)} %get-tuple-element.15), channel_id=1, source_target_pairs={{8,0},{16,8},{24,16},{32,24},{40,32},{48,40},{56,48},{64,56},{72,6... | collective-permute-start | bytes 1572872 | tf_op jit(solution)/shard_map/ppermute | solution.py:193
  161.4 26.4 %collective-permute-start.1 = (f32[128,1024]{1,0:T(8,128)S(1)}, f32[128,1024]{1,0:T(8,128)S(1)}, u32[]{:S(2)}, u32[]{:S(2)}) collective-permute-start(f32[128,1024]{1,0:T(8,128)S(1)} %select_add_fusion.1), channel_id=1, source_target_pairs={{16,0},{24,8},{32,16},{40,24},{48,32},{56,40},{64,48},{72,56},{80,... | collective-permute-start | bytes 1572872 | tf_op jit(solution)/shard_map/ppermute | solution.py:193
  189.7 130.9 %all-gather.16.cloned.1.call-start = ((), (), s32[]{:S(2)}) async-start(), calls=%async_computation.4 | async-start | bytes 4718592 | tf_op jit(solution)/shard_map/all_gather | solution.py:223
  189.8 24.7 %collective-permute-start.2 = (f32[128,2048]{1,0:T(8,128)S(1)}, f32[128,2048]{1,0:T(8,128)S(1)}, u32[]{:S(2)}, u32[]{:S(2)}) collective-permute-start(f32[128,2048]{1,0:T(8,128)S(1)} %get-tuple-element.18), channel_id=1, source_target_pairs={{8,0},{16,8},{24,16},{32,24},{40,32},{48,40},{56,48},{64,56},{72,6... | collective-permute-start | bytes 3145736 | tf_op jit(solution)/shard_map/ppermute | solution.py:193
  214.6 48.7 %collective-permute-start.3 = (f32[128,2048]{1,0:T(8,128)S(1)}, f32[128,2048]{1,0:T(8,128)S(1)}, u32[]{:S(2)}, u32[]{:S(2)}) collective-permute-start(f32[128,2048]{1,0:T(8,128)S(1)} %select_add_fusion), channel_id=1, source_target_pairs={{16,0},{24,8},{32,16},{40,24},{48,32},{56,40},{64,48},{72,56},{80,... | collective-permute-start | bytes 3145736 | tf_op jit(solution)/shard_map/ppermute | solution.py:193
  264.5 2.2 copy-start.2
  318.7 2.0 copy-start.6
  320.6 2.2 copy-start.3
  322.8 2.2 copy-start.7
Sparse Core Ops, SparseCore 0:
  10.4 38.8 all-gather.7
  51.7 34.5 all-gather.9
  88.8 34.5 all-gather.11
  189.9 36.3 all-gather.13
  264.6 41.9 all-gather.15
